TPU v7x, 32 devices: a whole 2x2x4 slice. The times are simulated.
32 devices in a mesh: groups: 2 (over y), blk: 4 (over x, core), branch: 4 (over z).
Axes of the slice: x: 2, y: 2, z: 4, core: 2. Of those that a mesh axis runs over, the one named last changes fastest.
Arguments:
- queries: bfloat16 [128, 64, 128], P(('groups', 'blk', 'branch')), parts along dimension 0, may hold values from -128 to 128
- new_keys: bfloat16 [128, 8, 128], P(('groups', 'blk', 'branch')), parts along dimension 0, may hold values from -8 to 8
- fresh_token_values: bfloat16 [128, 8, 128], P(('groups', 'blk', 'branch')), parts along dimension 0, may hold values from -6 to 6
- prefix_keys: bfloat16 [16384, 8, 128], P(('groups', 'blk'), 'branch'), parts along dimension 0, may hold values from -4 to 4
- prefix_values: bfloat16 [16384, 8, 128], P(('groups', 'blk'), 'branch'), parts along dimension 0, may hold values from -6 to 6
- suffix_keys: bfloat16 [128, 512, 8, 128], P(('groups', 'blk'), None, 'branch'), parts along dimension 0, may hold values from -8 to 8
- suffix_values: bfloat16 [128, 512, 8, 128], P(('groups', 'blk'), None, 'branch'), parts along dimension 0, may hold values from -6 to 6
- suffix_lengths: int32 [128], P('groups'), parts along dimension 0, may hold values from 1 to 512, 20480 in all
- slot_branch: int32 [128], P('groups'), parts along dimension 0, may hold values from 0 to 63, as said below
Outputs:
- attended: bfloat16 [128, 64, 128], P(('groups', 'blk', 'branch')), parts along dimension 0
There are 2 independent parts, one for each index of `groups`. A program takes and returns all parts, laid end to end along the dimension named above; each array names one. Nothing has to cross between parts.
Inputs may be any that keep to these rules, and one draw needn't show every extreme that they name: slot_branch is a permutation that maps each aligned block of 16 slots onto the branches of the same block of 16 branches.
All inputs are finite; a program needn't handle non-finite values.
Results may differ from a plain program's by a relative error of at most 0.0045.
Values may be sent and summed in bfloat16 or wider, within the bound.
A program may use at most 128 MiB of HBM per device.

v0:
```python
import math

import jax
import jax.numpy as jnp
from jax import lax
from jax.sharding import PartitionSpec as P

neg_large = -1e30


def advance(carried, scores, apply_values):
    out_sum, top_score, weight_sum = carried
    new_top = jnp.maximum(top_score, jnp.max(scores, axis=-1))
    rescale = jnp.exp(top_score - new_top)
    weights = jnp.exp(scores - new_top[..., None])
    weight_sum = weight_sum * rescale + jnp.sum(weights, axis=-1)
    out_sum = out_sum * rescale[..., None] + apply_values(weights.astype(jnp.bfloat16))
    return (out_sum, new_top, weight_sum)


def combine(first, second):
    top_score = jnp.maximum(first[1], second[1])
    scale_one = jnp.exp(first[1] - top_score)
    scale_two = jnp.exp(second[1] - top_score)
    out_sum = first[0] * scale_one[..., None] + second[0] * scale_two[..., None]
    weight_sum = first[2] * scale_one + second[2] * scale_two
    return (out_sum, top_score, weight_sum)


def empty_state(rows, kv_heads, group, head_dim):
    return (
        jnp.zeros((rows, kv_heads, group, head_dim), jnp.float32),
        jnp.full((rows, kv_heads, group), neg_large, jnp.float32),
        jnp.zeros((rows, kv_heads, group), jnp.float32),
    )


def attend_prefix(carried, query_rows, key_rows, value_rows):
    total = key_rows.shape[0]
    kv_heads, head_dim = (key_rows.shape[1], key_rows.shape[2])
    width = math.gcd(total, 512)
    count = total // width
    score_scale = 1.0 / math.sqrt(head_dim)
    key_blocks = key_rows.reshape(count, width, kv_heads, head_dim)
    value_blocks = value_rows.reshape(count, width, kv_heads, head_dim)

    def step(state, blocks):
        key_block, value_block = blocks
        scores = (
            jnp.einsum("rkgd,nkd->rkgn", query_rows, key_block, preferred_element_type=jnp.float32)
            * score_scale
        )

        def apply_values(weights):
            return jnp.einsum(
                "rkgn,nkd->rkgd", weights, value_block, preferred_element_type=jnp.float32
            )

        return (advance(state, scores, apply_values), None)

    final_output, _ = lax.scan(step, carried, (key_blocks, value_blocks))
    return final_output


def attend_suffix(
    slot_queries, slot_new_keys, slot_new_values, suffix_keys, suffix_values, slot_lengths
):
    head_dim = slot_queries.shape[3]
    score_scale = 1.0 / math.sqrt(head_dim)
    own_score = (
        jnp.einsum("skgd,skd->skg", slot_queries, slot_new_keys, preferred_element_type=jnp.float32)
        * score_scale
    )
    own_value = jnp.broadcast_to(
        slot_new_values.astype(jnp.float32)[:, :, None, :], slot_queries.shape
    )
    carried = (own_value, own_score, jnp.ones_like(own_score))
    scores = (
        jnp.einsum("skgd,snkd->skgn", slot_queries, suffix_keys, preferred_element_type=jnp.float32)
        * score_scale
    )
    positions = jnp.arange(suffix_keys.shape[1], dtype=jnp.int32)
    valid_mask = positions[None, :] < slot_lengths[:, None]
    scores = jnp.where(valid_mask[:, None, None, :], scores, neg_large)

    def apply_values(weights):
        return jnp.einsum(
            "skgn,snkd->skgd", weights, suffix_values, preferred_element_type=jnp.float32
        )

    return advance(carried, scores, apply_values)


def per_device(
    queries,
    new_keys,
    fresh_token_values,
    prefix_keys,
    prefix_values,
    suffix_keys,
    suffix_values,
    suffix_lengths,
    slot_branch,
):
    head_rows, nearby_keys, nearby_values = (
        lax.all_to_all(queries, "branch", split_axis=1, concat_axis=0, tiled=True),
        lax.all_to_all(new_keys, "branch", split_axis=1, concat_axis=0, tiled=True),
        lax.all_to_all(fresh_token_values, "branch", split_axis=1, concat_axis=0, tiled=True),
    )
    rows = head_rows.shape[0]
    local_key_value = nearby_keys.shape[1]
    head_dim = nearby_keys.shape[2]
    group = head_rows.shape[1] // local_key_value
    query_rows = head_rows.reshape(rows, local_key_value, group, head_dim)
    block_index = lax.axis_index("blk")
    first_row = block_index * rows
    pieces = lax.all_gather(head_rows, "blk", axis=0, tiled=True)
    count = pieces.shape[0]
    fresh = attend_prefix(
        empty_state(count, local_key_value, group, head_dim),
        pieces.reshape(count, local_key_value, group, head_dim),
        prefix_keys,
        prefix_values,
    )
    full_state = tuple((member for member in fresh))
    out_parts, top_parts, sum_parts = (
        lax.all_to_all(full_state[0][None], "blk", split_axis=1, concat_axis=0, tiled=True),
        lax.all_to_all(full_state[1][None], "blk", split_axis=1, concat_axis=0, tiled=True),
        lax.all_to_all(full_state[2][None], "blk", split_axis=1, concat_axis=0, tiled=True),
    )
    top_score = jnp.max(top_parts, axis=0)
    rescale = jnp.exp(top_parts - top_score[None])
    prefix_state = (
        jnp.sum(out_parts * rescale[..., None], axis=0),
        top_score,
        jnp.sum(sum_parts * rescale, axis=0),
    )
    local_slot_index = lax.dynamic_slice_in_dim(slot_branch, first_row, rows) - first_row
    length_block = lax.dynamic_slice_in_dim(suffix_lengths, first_row, rows)
    picker = local_slot_index[:, None] == jnp.arange(rows, dtype=jnp.int32)[None, :]
    select_halfway = picker.astype(jnp.bfloat16)
    slot_queries = jnp.einsum(
        "sb,bkgd->skgd", select_halfway, query_rows, preferred_element_type=jnp.float32
    ).astype(jnp.bfloat16)
    slot_new_keys = jnp.einsum(
        "qx,xuy->quy", select_halfway, nearby_keys, preferred_element_type=jnp.float32
    ).astype(jnp.bfloat16)
    slot_new_values = jnp.einsum(
        "qx,xuy->quy", select_halfway, nearby_values, preferred_element_type=jnp.float32
    ).astype(jnp.bfloat16)
    slot_lengths = jnp.sum(jnp.where(picker, length_block[None, :], 0), axis=1)
    slot_state = attend_suffix(
        slot_queries, slot_new_keys, slot_new_values, suffix_keys, suffix_values, slot_lengths
    )
    pick_wide = picker.astype(jnp.float32)
    suffix_state = (
        jnp.einsum("sb,skgd->bkgd", pick_wide, slot_state[0], precision=lax.Precision.HIGHEST),
        jnp.einsum("sb,skg->bkg", pick_wide, slot_state[1], precision=lax.Precision.HIGHEST),
        jnp.einsum("sb,skg->bkg", pick_wide, slot_state[2], precision=lax.Precision.HIGHEST),
    )
    out_sum, top_score, weight_sum = combine(prefix_state, suffix_state)
    final_output = (out_sum / weight_sum[..., None]).astype(jnp.bfloat16)
    final_output = final_output.reshape(rows, local_key_value * group, head_dim)
    return lax.all_to_all(final_output, "branch", split_axis=0, concat_axis=1, tiled=True)


def solution(mesh):
    return jax.shard_map(
        per_device,
        mesh=mesh,
        in_specs=(
            P(("groups", "blk", "branch"), None, None),
            P(("groups", "blk", "branch"), None, None),
            P(("groups", "blk", "branch"), None, None),
            P(("groups", "blk"), "branch", None),
            P(("groups", "blk"), "branch", None),
            P(("groups", "blk"), None, "branch", None),
            P(("groups", "blk"), None, "branch", None),
            P("groups"),
            P("groups"),
        ),
        out_specs=P(("groups", "blk", "branch"), None, None),
        check_vma=False,
    )
```

profile of v0, /device:TPU:0, one launch (start us, length us, event | category | flops | bytes accessed | tf_op | source)
XLA Modules:
  0.0 90.6 jit_solution(9462983046000429940)
XLA Ops:
  0.0 1.3 %copy.68 = bf16[4,8,128]{2,0,1:T(4,128)(2,1)} copy(bf16[4,8,128]{2,1,0:T(8,128)(2,1)} %param.13) | data formatting | bytes 16384 | tf_op args[2]
  1.3 6.3 %all-to-all-start.4 = ((bf16[4,8,128]{2,0,1:T(4,128)(2,1)}), bf16[4,8,128]{2,0,1:T(4,128)(2,1)S(1)}, u32[]{:S(2)}, u32[]{:S(2)}) async-start(bf16[4,8,128]{2,0,1:T(4,128)(2,1)} %copy.68), calls=%async_computation.4 | async-start | bytes 16384 | tf_op jit(solution)/shard_map/all_to_all | solution.py:108
  7.6 0.7 dynamic-slice_subtract_fusion
  8.4 0.7 dynamic_slice.14
  9.4 1.3 %copy.60 = bf16[4,8,128]{2,0,1:T(4,128)(2,1)} copy(bf16[4,8,128]{2,1,0:T(8,128)(2,1)} %param.12) | data formatting | bytes 16384 | tf_op args[1]
  10.7 1.5 %copy.53 = bf16[4,64,128]{2,0,1:T(4,128)(2,1)} copy(bf16[4,64,128]{2,1,0:T(8,128)(2,1)} %param.11) | data formatting | bytes 131072 | tf_op args[0]
  12.2 1.1 %all-to-all-done.4 = bf16[4,8,128]{2,0,1:T(4,128)(2,1)S(1)} async-done(((bf16[4,8,128]{2,0,1:T(4,128)(2,1)}), bf16[4,8,128]{2,0,1:T(4,128)(2,1)S(1)}, u32[]{:S(2)}, u32[]{:S(2)}) %all-to-all-start.4) | async-done | bytes 8224 | tf_op jit(solution)/shard_map/all_to_all | solution.py:108
  13.2 4.0 %all-to-all-start.3 = ((bf16[4,8,128]{2,0,1:T(4,128)(2,1)}), bf16[4,8,128]{2,0,1:T(4,128)(2,1)S(1)}, u32[]{:S(2)}, u32[]{:S(2)}) async-start(bf16[4,8,128]{2,0,1:T(4,128)(2,1)} %copy.60), calls=%async_computation.3 | async-start | bytes 16384 | tf_op jit(solution)/shard_map/all_to_all | solution.py:107
  17.5 5.4 %all-to-all-done.3 = bf16[4,8,128]{2,0,1:T(4,128)(2,1)S(1)} async-done(((bf16[4,8,128]{2,0,1:T(4,128)(2,1)}), bf16[4,8,128]{2,0,1:T(4,128)(2,1)S(1)}, u32[]{:S(2)}, u32[]{:S(2)}) %all-to-all-start.3) | async-done | bytes 8224 | tf_op jit(solution)/shard_map/all_to_all | solution.py:107
  22.9 3.3 %all-to-all-start = ((bf16[4,64,128]{2,0,1:T(4,128)(2,1)}), bf16[4,64,128]{2,0,1:T(4,128)(2,1)S(1)}, u32[]{:S(2)}, u32[]{:S(2)}) async-start(bf16[4,64,128]{2,0,1:T(4,128)(2,1)} %copy.53), calls=%async_computation | async-start | bytes 131072 | tf_op jit(solution)/shard_map/all_to_all | solution.py:106
  26.4 5.5 %all-to-all-done = bf16[4,64,128]{2,0,1:T(4,128)(2,1)S(1)} async-done(((bf16[4,64,128]{2,0,1:T(4,128)(2,1)}), bf16[4,64,128]{2,0,1:T(4,128)(2,1)S(1)}, u32[]{:S(2)}, u32[]{:S(2)}) %all-to-all-start) | async-done | bytes 65568 | tf_op jit(solution)/shard_map/all_to_all | solution.py:106
  32.1 5.8 %all_gather.3 = bf16[64,16,128]{2,0,1:T(8,128)(2,1)S(1)} all-gather(bf16[16,16,128]{2,0,1:T(8,128)(2,1)S(1)} %bitcast.122), channel_id=1, replica_groups=mesh['groups'=2,'blk'=4,'branch'=4] {'blk'}, dimensions={0}, use_global_device_ids=true | all-gather | bytes 327680 | tf_op jit(solution)/shard_map/all_gather | solution.py:117
  37.9 13.3 %while.15 = (s32[]{:T(128)}, f32[64,2,8,128]{3,0,2,1:T(8,128)S(1)}, f32[64,2,8]{0,2,1:T(8,128)S(1)}, f32[64,2,8]{0,2,1:T(8,128)S(1)}, bf16[4,512,2,128]{3,2,1,0:...) while((s32[]{:T(128)}, f32[64,2,8,128]{3,0,2,1:T(8,128)S(1)}, ...), condition=%wide.region_3.4_spmd.clone, body=%wide.region_0.3_spmd.clone.sunk | while | flops 273028096 | bytes 9240693 | solution.py:61
  37.9 1.4 %constant_dynamic-slice_fusion.3 = (bf16[1,512,2,128]{3,2,1,0:T(2,128)(2,1)S(1)}, bf16[1,512,2,128]{3,2,1,0:T(2,128)(2,1)S(1)}) fusion(bf16[4,512,2,128]{3,2,1,0:T(2,128)(2,1)} %get-tuple-element.199, s32[]{:T(128)S(6)} %copy.133, bf16[4,512,2,128]{3,2,1,0:T(2,128)(2,1)} %get-tuple-element.197), kind=kLoop, calls=%fused_computation.17.clone.1 | loop fusion | bytes 1048580 | tf_op jit(solution)/shard_map/while/body/jit(dynamic_index_in_dim)/dynamic_slice | solution.py:61
  40.4 0.8 fusion.70
  41.2 1.4 %constant_dynamic-slice_fusion.3 = (bf16[1,512,2,128]{3,2,1,0:T(2,128)(2,1)S(1)}, bf16[1,512,2,128]{3,2,1,0:T(2,128)(2,1)S(1)}) fusion(bf16[4,512,2,128]{3,2,1,0:T(2,128)(2,1)} %get-tuple-element.199, s32[]{:T(128)S(6)} %copy.133, bf16[4,512,2,128]{3,2,1,0:T(2,128)(2,1)} %get-tuple-element.197), kind=kLoop, calls=%fused_computation.17.clone.1 | loop fusion | bytes 1048580 | tf_op jit(solution)/shard_map/while/body/jit(dynamic_index_in_dim)/dynamic_slice | solution.py:61
  43.8 0.8 fusion.70
  44.6 1.4 %constant_dynamic-slice_fusion.3 = (bf16[1,512,2,128]{3,2,1,0:T(2,128)(2,1)S(1)}, bf16[1,512,2,128]{3,2,1,0:T(2,128)(2,1)S(1)}) fusion(bf16[4,512,2,128]{3,2,1,0:T(2,128)(2,1)} %get-tuple-element.199, s32[]{:T(128)S(6)} %copy.133, bf16[4,512,2,128]{3,2,1,0:T(2,128)(2,1)} %get-tuple-element.197), kind=kLoop, calls=%fused_computation.17.clone.1 | loop fusion | bytes 1048580 | tf_op jit(solution)/shard_map/while/body/jit(dynamic_index_in_dim)/dynamic_slice | solution.py:61
  47.1 0.8 fusion.70
  47.9 1.4 %constant_dynamic-slice_fusion.3 = (bf16[1,512,2,128]{3,2,1,0:T(2,128)(2,1)S(1)}, bf16[1,512,2,128]{3,2,1,0:T(2,128)(2,1)S(1)}) fusion(bf16[4,512,2,128]{3,2,1,0:T(2,128)(2,1)} %get-tuple-element.199, s32[]{:T(128)S(6)} %copy.133, bf16[4,512,2,128]{3,2,1,0:T(2,128)(2,1)} %get-tuple-element.197), kind=kLoop, calls=%fused_computation.17.clone.1 | loop fusion | bytes 1048580 | tf_op jit(solution)/shard_map/while/body/jit(dynamic_index_in_dim)/dynamic_slice | solution.py:61
  50.4 0.8 fusion.70
  51.4 0.7 reshape.83
  52.1 3.2 %all-to-all-start.5 = ((f32[4,1,256]{2,1,0:T(1,128)}), f32[4,1,256]{2,1,0:T(1,128)S(1)}, u32[]{:S(2)}, u32[]{:S(2)}) async-start(f32[4,1,256]{2,1,0:T(1,128)} %reshape.83), calls=%async_computation.5 | async-start | bytes 8192 | tf_op jit(solution)/shard_map/all_to_all | solution.py:129
  55.6 3.5 %fusion.56 = (f32[16,2,8]{2,1,0:T(2,128)S(1)}, f32[16,2,8,512]{3,2,1,0:T(8,128)S(1)}) fusion(bf16[16,512,2,128]{3,2,1,0:T(2,128)(2,1)} %param.16, bf16[16,2,8,128]{3,0,2,1:T(8,128)(2,1)S(1)} %convolution_convert_fusion, pred[16,512]{1,0:T(8,128)(4,1)S(1)} %iota_compare_fusion), kind=kOutput, calls=%fused_computation.75 | convolution fusion | flops 33947392 | bytes 4793344 | tf_op jit(solution)/shard_map/skgd,snkd->skgn/dot_general | solution.py:79
  59.4 0.7 reshape.81
  60.2 3.3 %all-to-all-start.2 = ((f32[4,1,256]{2,1,0:T(1,128)}), f32[4,1,256]{2,1,0:T(1,128)S(1)}, u32[]{:S(2)}, u32[]{:S(2)}) async-start(f32[4,1,256]{2,1,0:T(1,128)} %reshape.81), calls=%async_computation.2 | async-start | bytes 8192 | tf_op jit(solution)/shard_map/all_to_all | solution.py:128
  63.4 2.9 %fusion.20 = f32[16,2,8,128]{3,2,1,0:T(8,128)S(1)} fusion(bf16[16,512,2,128]{3,2,1,0:T(2,128)(2,1)} %param.17, f32[16,2,8,512]{3,2,1,0:T(8,128)S(1)} %get-tuple-element.119, f32[16,2,8]{2,1,0:T(2,128)S(1)} %multiply_maximum_fusion, f32[16,2,8]{2,1,0:T(2,128)S(1)} %get-tuple-element.111, f32[16,2,128]{2,1,0:T(2,128)S(1)} %copy.70), kind=kOutput, calls=%fused_computation.26 | convolution fusion | flops 33882112 | bytes 4868096 | tf_op jit(solution)/shard_map/skgn,snkd->skgd/dot_general | solution.py:87
  66.5 1.1 %copy.124 = f32[64,2,8,128]{3,2,1,0:T(8,128)} copy(f32[64,2,8,128]{3,0,2,1:T(8,128)S(1)} %get-tuple-element.44) | data formatting | bytes 1048576 | tf_op jit(solution)/shard_map/while | solution.py:61
  68.9 3.5 %all-to-all-start.1 = ((f32[1,64,2,8,128]{4,3,2,0,1:T(8,128)}), f32[1,64,2,8,128]{4,3,2,0,1:T(8,128)S(1)}, u32[]{:S(2)}, u32[]{:S(2)}) async-start(f32[1,64,2,8,128]{4,3,2,0,1:T(8,128)} %bitcast.100), calls=%async_computation.1 | async-start | bytes 1048576 | tf_op jit(solution)/shard_map/all_to_all | solution.py:127
  72.4 0.7 reduce.1
  73.9 7.3 %all-to-all-done.1 = f32[1,64,2,8,128]{4,3,2,0,1:T(8,128)S(1)} async-done(((f32[1,64,2,8,128]{4,3,2,0,1:T(8,128)}), f32[1,64,2,8,128]{4,3,2,0,1:T(8,128)S(1)}, u32[]{:S(2)}, u32[]{:S(2)}) %all-to-all-start.1) | async-done | bytes 524320 | tf_op jit(solution)/shard_map/all_to_all | solution.py:127
  81.8 8.1 %all_to_all.108 = bf16[16,16,128]{2,1,0:T(8,128)(2,1)S(1)} all-to-all(bf16[16,16,128]{2,1,0:T(8,128)(2,1)S(1)} %copy.77), channel_id=1, replica_groups=mesh['groups'=2,'blk'=4,'branch'=4] {'branch'}, dimensions={0} | all-to-all | bytes 131072 | tf_op jit(solution)/shard_map/all_to_all | solution.py:164
  (58 shorter events, 9.5 us)
Async XLA Ops:
  1.3 11.9 %all-to-all-start.4 = ((bf16[4,8,128]{2,0,1:T(4,128)(2,1)}), bf16[4,8,128]{2,0,1:T(4,128)(2,1)S(1)}, u32[]{:S(2)}, u32[]{:S(2)}) async-start(bf16[4,8,128]{2,0,1:T(4,128)(2,1)} %copy.68), calls=%async_computation.4 | async-start | bytes 16384 | tf_op jit(solution)/shard_map/all_to_all | solution.py:108
  13.2 9.6 %all-to-all-start.3 = ((bf16[4,8,128]{2,0,1:T(4,128)(2,1)}), bf16[4,8,128]{2,0,1:T(4,128)(2,1)S(1)}, u32[]{:S(2)}, u32[]{:S(2)}) async-start(bf16[4,8,128]{2,0,1:T(4,128)(2,1)} %copy.60), calls=%async_computation.3 | async-start | bytes 16384 | tf_op jit(solution)/shard_map/all_to_all | solution.py:107
  22.9 9.0 %all-to-all-start = ((bf16[4,64,128]{2,0,1:T(4,128)(2,1)}), bf16[4,64,128]{2,0,1:T(4,128)(2,1)S(1)}, u32[]{:S(2)}, u32[]{:S(2)}) async-start(bf16[4,64,128]{2,0,1:T(4,128)(2,1)} %copy.53), calls=%async_computation | async-start | bytes 131072 | tf_op jit(solution)/shard_map/all_to_all | solution.py:106
  52.1 8.1 %all-to-all-start.5 = ((f32[4,1,256]{2,1,0:T(1,128)}), f32[4,1,256]{2,1,0:T(1,128)S(1)}, u32[]{:S(2)}, u32[]{:S(2)}) async-start(f32[4,1,256]{2,1,0:T(1,128)} %reshape.83), calls=%async_computation.5 | async-start | bytes 8192 | tf_op jit(solution)/shard_map/all_to_all | solution.py:129
  60.2 8.8 %all-to-all-start.2 = ((f32[4,1,256]{2,1,0:T(1,128)}), f32[4,1,256]{2,1,0:T(1,128)S(1)}, u32[]{:S(2)}, u32[]{:S(2)}) async-start(f32[4,1,256]{2,1,0:T(1,128)} %reshape.81), calls=%async_computation.2 | async-start | bytes 8192 | tf_op jit(solution)/shard_map/all_to_all | solution.py:128
  68.9 12.3 %all-to-all-start.1 = ((f32[1,64,2,8,128]{4,3,2,0,1:T(8,128)}), f32[1,64,2,8,128]{4,3,2,0,1:T(8,128)S(1)}, u32[]{:S(2)}, u32[]{:S(2)}) async-start(f32[1,64,2,8,128]{4,3,2,0,1:T(8,128)} %bitcast.100), calls=%async_computation.1 | async-start | bytes 1048576 | tf_op jit(solution)/shard_map/all_to_all | solution.py:127
where the time goes:
time: 91.4 us; the launch traced here: 90.6 us
  starting transfers between devices  23.7 us (26%)
  waiting for transfers between devices  19.2 us (21%)
  local copies, waits for them, and re-layouts  15 us (16%)
  blocking collectives  13.9 us (15%)
  matrix products  13 us (14%)
  other arithmetic  5.34 us (6%)
    all_to_all x1, blocking collectives, per_device(): lax.all_to_all(final_output, 'branch', split_axis=0, concat_axis=1, tiled...  8.11 us
    all_to_all x1, waiting for transfers between devices, per_device(): lax.all_to_all(full_state[0][None], 'blk', split_axis=1, concat_axis=0, t...  7.27 us
    all_to_all x1, starting transfers between devices, per_device(): lax.all_to_all(fresh_token_values, 'branch', split_axis=1, concat_axis=0,...  6.35 us
    unnamed x9, local copies, waits for them, and re-layouts  5.89 us
    all_gather x1, blocking collectives, per_device(): pieces = lax.all_gather(head_rows, 'blk', axis=0, tiled=True)  5.78 us
    dynamic_slice x4, local copies, waits for them, and re-layouts, attend_prefix(): final_output, _ = lax.scan(step, carried, (key_blocks, value_blocks))  5.58 us
    all_to_all x1, waiting for transfers between devices, per_device(): lax.all_to_all(queries, 'branch', split_axis=1, concat_axis=0, tiled=True)  5.51 us
    all_to_all x1, waiting for transfers between devices, per_device(): lax.all_to_all(new_keys, 'branch', split_axis=1, concat_axis=0, tiled=True)  5.38 us
  transfers between devices with their start and end apart: 6, of which 4 were waited for; matrix products, arithmetic and copies ran while one was open for 18% of the time, Pallas kernels for 0%

commit v1 on v0

v1 whole, which is shorter than its diff:
```python
import functools
import math

import jax
import jax.numpy as jnp
from jax import lax
from jax.experimental import pallas as pl
from jax.experimental.pallas import tpu as pltpu
from jax.sharding import PartitionSpec as P

MESH = pl.DeviceIdType.MESH
F32 = jnp.float32
BF16 = jnp.bfloat16
STAT_ROWS = 16


def kernel(
    cfg,
    q_hbm,
    nk_hbm,
    nv_hbm,
    pk_hbm,
    pv_hbm,
    sk_hbm,
    sv_hbm,
    len_hbm,
    slot_hbm,
    out_ref,
    q_own,
    nk,
    nv,
    pk_raw,
    pv_raw,
    pk_wide,
    pv_wide,
    pk,
    pv,
    sk,
    sv,
    lens,
    slots,
    q_all,
    part_o,
    part_m,
    part_l,
    own_w,
    own_v,
    send_buf,
    recv_buf,
    local_sem,
    send_q,
    recv_q,
    send_p,
    recv_p,
):
    nblk, nbr, rdev, kvl, group, hd, keys, suf = cfg
    n = nblk * nbr
    rows = rdev * nbr
    mrow = rdev * group
    factor = math.log2(math.e) / math.sqrt(hd)
    grp = lax.axis_index("groups")
    my_blk = lax.axis_index("blk")
    my_br = lax.axis_index("branch")
    me = my_blk * nbr + my_br

    def device(p):
        return (grp, lax.div(p, nbr), lax.rem(p, nbr))

    pairs = [
        (q_hbm, q_own),
        (nk_hbm, nk),
        (nv_hbm, nv),
        (pk_hbm, pk_raw),
        (pv_hbm, pv_raw),
        (len_hbm, lens),
        (slot_hbm, slots),
        (sk_hbm, sk),
        (sv_hbm, sv),
    ]
    local = [pltpu.make_async_copy(a, b, local_sem.at[i]) for i, (a, b) in enumerate(pairs)]
    own_q = pltpu.make_async_copy(
        q_hbm.at[:, my_br], q_all.at[pl.ds(me * rdev, rdev)], local_sem.at[len(pairs)]
    )

    barrier = pltpu.get_barrier_semaphore()

    def greet(k, c):
        pl.semaphore_signal(
            barrier, inc=1, device_id=device(lax.rem(me + k, n)), device_id_type=MESH
        )
        return c

    lax.fori_loop(1, n, greet, 0)
    for copy in local[:5]:
        copy.start()
    own_q.start()
    for copy in local[5:]:
        copy.start()
    pl.semaphore_wait(barrier, n - 1)

    def q_copy(p, source):
        return pltpu.make_async_remote_copy(
            src_ref=q_hbm.at[:, lax.rem(p, nbr)],
            dst_ref=q_all.at[pl.ds(source * rdev, rdev)],
            send_sem=send_q.at[p],
            recv_sem=recv_q.at[source],
            device_id=device(p),
            device_id_type=MESH,
        )

    def send_one(k, c):
        q_copy(lax.rem(me + k, n), me).start()
        return c

    lax.fori_loop(1, n, send_one, 0)

    def p_copy(p, source):
        return pltpu.make_async_remote_copy(
            src_ref=send_buf.at[p],
            dst_ref=recv_buf.at[source],
            send_sem=send_p.at[p],
            recv_sem=recv_p.at[source],
            device_id=device(p),
            device_id_type=MESH,
        )

    local[3].wait()
    local[4].wait()
    chunk = math.gcd(keys, 256)

    def spread(t, c):
        at = pl.ds(pl.multiple_of(t * chunk * kvl, chunk * kvl), chunk * kvl)
        for raw, wide, dest in ((pk_raw, pk_wide, pk), (pv_raw, pv_wide, pv)):
            wide[at, :] = raw[at, :].astype(F32)
            for h in range(kvl):
                piece = wide[pl.ds(t * chunk * kvl + h, chunk, stride=kvl), :]
                dest[h, pl.ds(pl.multiple_of(t * chunk, chunk), chunk), :] = piece.astype(BF16)
        return c

    lax.fori_loop(0, keys // chunk, spread, 0)

    for copy in local[:3]:
        copy.wait()
    nk_wide = nk[...].astype(F32)
    nv_wide = nv[...].astype(F32)
    for jj in range(nbr):
        q_wide = q_own[:, jj].astype(F32)
        for h in range(kvl):
            head = jj * kvl + h
            key = nk_wide[:, head : head + 1, :]
            value = nv_wide[:, head : head + 1, :]
            part = q_wide[:, h * group : (h + 1) * group, :]
            score = jnp.sum(part * key, axis=-1, keepdims=True)
            own_w[jj, h] = jnp.broadcast_to(score, (rdev, group, hd)).reshape(mrow, hd)
            own_v[jj, h] = jnp.broadcast_to(value, (rdev, group, hd)).reshape(mrow, hd)

    lane = lax.broadcasted_iota(jnp.int32, (mrow, hd), 1)
    line = lax.broadcasted_iota(jnp.int32, (mrow, hd), 0)
    picks = [lane == line + h * mrow for h in range(kvl)]
    stat_line = lax.broadcasted_iota(jnp.int32, (STAT_ROWS, hd), 0)

    def to_row(columns):
        total = None
        for h in range(kvl):
            one = jnp.sum(jnp.where(picks[h], columns[h], 0.0), axis=0, keepdims=True)
            total = one if total is None else total + one
        return total

    def split(x):
        high = x.astype(BF16).astype(F32)
        rest = x - high
        mid = rest.astype(BF16).astype(F32)
        return [high, mid, rest - mid]

    def build(p, outs, tops, sums):
        for h in range(kvl):
            send_buf[p, h * mrow : (h + 1) * mrow, :] = outs[h].astype(BF16)
        stats = jnp.zeros((STAT_ROWS, hd), F32)
        for i, piece in enumerate(split(to_row(tops)) + split(to_row(sums))):
            stats = jnp.where(stat_line == i, piece, stats)
        send_buf[p, kvl * mrow : kvl * mrow + STAT_ROWS, :] = stats.astype(BF16)

    half = nblk // 2
    my_chip = lax.div(my_blk, 2)
    my_core = lax.rem(my_blk, 2)

    def prefix_step(d, c):
        chip = lax.rem(my_chip + lax.div(d, 2), half)
        core = lax.rem(my_core + lax.rem(d, 2), 2)
        ib = chip * 2 + core

        @pl.when(d < nblk)
        def _():
            for jj in range(nbr):
                q_copy(me, ib * nbr + jj).wait_recv()

        @pl.when(d == nblk)
        def _():
            own_q.wait()
            for k in range(1, nbr):
                q_copy(me, my_blk * nbr + lax.rem(my_br + k, nbr)).wait_recv()

        q_wide = q_all[pl.ds(ib * rows, rows)].astype(F32)
        for h in range(kvl):
            query = q_wide[:, h * group : (h + 1) * group, :].reshape(rows * group, hd)
            scores = lax.dot_general(
                query.astype(BF16), pk[h], (((1,), (1,)), ((), ())), preferred_element_type=F32
            )
            top = jnp.max(scores, axis=1, keepdims=True)
            weights = jnp.exp2((scores - top) * factor)
            total = jnp.sum(weights, axis=1, keepdims=True)
            part_o[h] = jnp.dot(weights.astype(BF16), pv[h], preferred_element_type=F32)
            part_m[h] = jnp.broadcast_to(top, (rows * group, hd))
            part_l[h] = jnp.broadcast_to(total, (rows * group, hd))

        @pl.when(d < nblk)
        def _():
            for jj in range(nbr):
                at = slice(jj * mrow, (jj + 1) * mrow)
                p = ib * nbr + jj
                build(
                    p,
                    [part_o[h, at, :] for h in range(kvl)],
                    [part_m[h, at, :] for h in range(kvl)],
                    [part_l[h, at, :] for h in range(kvl)],
                )
                p_copy(p, me).start()

        return c

    lax.fori_loop(1, nblk + 1, prefix_step, 0)

    for copy in local[5:]:
        copy.wait()
    first = my_blk * rows
    qrow = kvl * group
    wide = suf * kvl
    col = lax.broadcasted_iota(jnp.int32, (qrow, wide), 1)
    row_head = lax.div(lax.broadcasted_iota(jnp.int32, (qrow, wide), 0), group)
    right_head = lax.rem(col, kvl) == row_head
    position = lax.div(col, kvl)

    def suffix_step(k, c):
        jj = lax.rem(my_br + k, nbr)
        keep = []
        for r in range(rdev):
            b = jj * rdev + r
            slot = jnp.int32(0)
            for s in range(rows):
                slot = jnp.where(slots[first + s] == first + b, s, slot)
            scores = lax.dot_general(
                q_all[first + b], sk[slot], (((1,), (1,)), ((), ())), preferred_element_type=F32
            )
            valid = right_head & (position < lens[first + b])
            keep.append((jnp.where(valid, scores, -1e30), slot))
        done = []
        for scores, slot in keep:
            top = jnp.max(scores, axis=1, keepdims=True)
            weights = jnp.exp2((scores - top) * factor)
            total = jnp.sum(weights, axis=1, keepdims=True)
            out = jnp.dot(weights.astype(BF16), sv[slot], preferred_element_type=F32)
            done.append((out, jnp.broadcast_to(top, out.shape), jnp.broadcast_to(total, out.shape)))
        outs, tops, sums = [], [], []
        at = pl.ds(pl.multiple_of(jj * mrow, mrow), mrow)
        for h in range(kvl):
            cut = slice(h * group, (h + 1) * group)
            o2, m2, l2 = (
                jnp.concatenate([item[i][cut] for item in done], axis=0) for i in range(3)
            )
            o1, m1, l1 = part_o[h, at, :], part_m[h, at, :], part_l[h, at, :]
            top = jnp.maximum(m1, m2)
            one = jnp.exp2((m1 - top) * factor)
            two = jnp.exp2((m2 - top) * factor)
            outs.append(o1 * one + o2 * two)
            tops.append(top)
            sums.append(l1 * one + l2 * two)
        p = my_blk * nbr + jj
        build(p, outs, tops, sums)

        @pl.when(k < nbr)
        def _():
            p_copy(p, me).start()

        return c

    lax.fori_loop(1, nbr + 1, suffix_step, 0)
    recv_buf[me] = send_buf[me]

    def wait_one(k, c):
        p_copy(me, lax.rem(me + k, n)).wait_recv()
        return c

    lax.fori_loop(1, n, wait_one, 0)

    def merge(jj, c):
        finals = []
        stats = []
        for ii in range(nblk):
            block = recv_buf[ii * nbr + jj, kvl * mrow : kvl * mrow + STAT_ROWS, :].astype(F32)
            stats.append(
                (block[0:1] + block[1:2] + block[2:3], block[3:4] + block[4:5] + block[5:6])
            )
        for h in range(kvl):
            tops = [
                jnp.sum(jnp.where(picks[h], s[0], 0.0), axis=1, keepdims=True) for s in stats
            ]
            sums = [
                jnp.sum(jnp.where(picks[h], s[1], 0.0), axis=1, keepdims=True) for s in stats
            ]
            mine = own_w[jj, h]
            top = mine
            for t in tops:
                top = jnp.maximum(top, t)
            scale = jnp.exp2((mine - top) * factor)
            num = own_v[jj, h] * scale
            den = scale
            for ii in range(nblk):
                scale = jnp.exp2((tops[ii] - top) * factor)
                piece = recv_buf[ii * nbr + jj, h * mrow : (h + 1) * mrow, :].astype(F32)
                num = num + piece * scale
                den = den + sums[ii] * scale
            finals.append((num / den).reshape(rdev, group, hd))
        out_ref[:, jj] = jnp.concatenate(finals, axis=1).astype(BF16)
        return c

    lax.fori_loop(0, nbr, merge, 0)

    def drain(k, c):
        p = lax.rem(me + k, n)
        q_copy(p, me).wait_send()
        p_copy(p, me).wait_send()
        return c

    lax.fori_loop(1, n, drain, 0)


def solution(mesh):
    nblk, nbr = mesh.shape["blk"], mesh.shape["branch"]

    def per_device(q, nk, nv, pk, pv, sk, sv, lens, slots):
        rdev, heads, hd = q.shape
        keys, kvl = pk.shape[:2]
        nslot, suf = sk.shape[:2]
        hl = heads // nbr
        group = hl // kvl
        n = nblk * nbr
        rows = rdev * nbr
        mrow = rdev * group
        cfg = (nblk, nbr, rdev, kvl, group, hd, keys, suf)
        dma = pltpu.SemaphoreType.DMA
        out = pl.pallas_call(
            functools.partial(kernel, cfg),
            out_shape=jax.ShapeDtypeStruct((rdev, nbr, hl, hd), BF16),
            in_specs=[pl.BlockSpec(memory_space=pl.ANY)] * 9,
            out_specs=pl.BlockSpec(memory_space=pltpu.VMEM),
            scratch_shapes=[
                pltpu.VMEM((rdev, nbr, hl, hd), BF16),
                pltpu.VMEM(nk.shape, BF16),
                pltpu.VMEM(nv.shape, BF16),
                pltpu.VMEM((keys * kvl, hd), BF16),
                pltpu.VMEM((keys * kvl, hd), BF16),
                pltpu.VMEM((keys * kvl, hd), F32),
                pltpu.VMEM((keys * kvl, hd), F32),
                pltpu.VMEM((kvl, keys, hd), BF16),
                pltpu.VMEM((kvl, keys, hd), BF16),
                pltpu.VMEM((nslot, suf * kvl, hd), BF16),
                pltpu.VMEM((nslot, suf * kvl, hd), BF16),
                pltpu.SMEM(lens.shape, jnp.int32),
                pltpu.SMEM(slots.shape, jnp.int32),
                pltpu.VMEM((n * rdev, hl, hd), BF16),
                pltpu.VMEM((kvl, rows * group, hd), F32),
                pltpu.VMEM((kvl, rows * group, hd), F32),
                pltpu.VMEM((kvl, rows * group, hd), F32),
                pltpu.VMEM((nbr, kvl, mrow, hd), F32),
                pltpu.VMEM((nbr, kvl, mrow, hd), F32),
                pltpu.VMEM((n, kvl * mrow + STAT_ROWS, hd), BF16),
                pltpu.VMEM((n, kvl * mrow + STAT_ROWS, hd), BF16),
                dma((10,)),
                dma((n,)),
                dma((n,)),
                dma((n,)),
                dma((n,)),
            ],
            compiler_params=pltpu.CompilerParams(
                collective_id=0, has_side_effects=True, vmem_limit_bytes=60 * 1024 * 1024
            ),
            name="attend",
        )(
            q.reshape(rdev, nbr, hl, hd),
            nk,
            nv,
            pk.reshape(keys * kvl, hd),
            pv.reshape(keys * kvl, hd),
            sk.reshape(nslot, suf * kvl, hd),
            sv.reshape(nslot, suf * kvl, hd),
            lens,
            slots,
        )
        return out.reshape(rdev, heads, hd)

    return jax.shard_map(
        per_device,
        mesh=mesh,
        in_specs=(
            P(("groups", "blk", "branch"), None, None),
            P(("groups", "blk", "branch"), None, None),
            P(("groups", "blk", "branch"), None, None),
            P(("groups", "blk"), "branch", None),
            P(("groups", "blk"), "branch", None),
            P(("groups", "blk"), None, "branch", None),
            P(("groups", "blk"), None, "branch", None),
            P("groups"),
            P("groups"),
        ),
        out_specs=P(("groups", "blk", "branch"), None, None),
        check_vma=False,
    )
```

time: 91.4 us -> 26.2 us (0.29)
  Pallas kernels: 0 us -> 24.6 us
  starting transfers between devices: 23.7 us -> 0 us
  waiting for transfers between devices: 19.2 us -> 0 us
  blocking collectives: 13.9 us -> 0 us
  local copies, waits for them, and re-layouts: 15 us -> 1.47 us
  matrix products: 13 us -> 0 us
  other arithmetic: 5.34 us -> 0 us
    pallas_call x0 -> x1, Pallas kernels: none -> 24.6 us  [per_device(): pl.pallas_call(functools.partial(kernel, cfg), out_shape=jax.ShapeDtypeSt...]
    all_to_all x6 -> x0, starting transfers between devices: 23.7 us -> none  [the longest x1 6.35 us: per_device(): lax.all_to_all(fresh_token_values, 'branch', split_axis=1, concat_axis=0,...]
    all_to_all x6 -> x0, waiting for transfers between devices: 19.2 us -> none  [the longest x1 7.27 us: per_device(): lax.all_to_all(full_state[0][None], 'blk', split_axis=1, concat_axis=0, t...]
    dot_general x15 -> x0, matrix products: 12.6 us -> none  [the longest x1 3.47 us: attend_suffix(): jnp.einsum('skgd,snkd->skgn', slot_queries, suffix_keys, preferred_elemen...]
    all_to_all x1 -> x0, blocking collectives: 8.11 us -> none  [per_device(): lax.all_to_all(final_output, 'branch', split_axis=0, concat_axis=1, tiled...]
    dynamic_slice x5 -> x0, local copies, waits for them, and re-layouts: 6.31 us -> none  [the longest x4 5.58 us: attend_prefix(): final_output, _ = lax.scan(step, carried, (key_blocks, value_blocks))]
    all_gather x1 -> x0, blocking collectives: 5.78 us -> none  [per_device(): pieces = lax.all_gather(head_rows, 'blk', axis=0, tiled=True)]
    unnamed x9 -> x1, local copies, waits for them, and re-layouts: 5.89 us -> 1.47 us
  transfers between devices with their start and end apart: 6 -> 0, of which waited for: 4 -> 0; matrix products, arithmetic and copies ran while one was open for 18% -> 0% of each run, Pallas kernels for 0% -> 0%
where the time goes in v1:
time: 26.2 us; the launch traced here: 26.1 us
  Pallas kernels  24.6 us (94%)
  local copies, waits for them, and re-layouts  1.47 us (6%)
    pallas_call x1, Pallas kernels, per_device(): pl.pallas_call(functools.partial(kernel, cfg), out_shape=jax.ShapeDtypeSt...  24.6 us
    unnamed x1, local copies, waits for them, and re-layouts  1.47 us

profile of v1, /device:TPU:0, one launch (start us, length us, event | category | flops | bytes accessed | tf_op | source)
XLA Modules:
  0.0 26.1 jit_solution(11179019053556973965)
XLA Ops:
  0.0 24.6 %attend.1 = bf16[4,4,16,128]{3,2,1,0:T(8,128)(2,1)} custom-call(bf16[4,4,16,128]{3,2,1,0:T(8,128)(2,1)} %bitcast.11, bf16[4,8,128]{2,1,0:T(8,128)(2,1)} %nk_hbm.1, bf16[4,8,128]{2,1,0:T(8,128)(2,1)} %nv_hbm.1, bf16[4096,128]{1,0:T(8,128)(2,1)} %bitcast.8, bf16[4096,128]{1,0:T(8,128)(2,1)} %bitcast.9, bf16[16,1024,128]{2,1,0:T(8,128)(2,1)} %bitcast.6, ...), custom_call_target="tpu_custom_call" | custom-call | tf_op jit(solution)/shard_map/attend/pallas_call | solution.py:351
  24.6 1.5 %copy.11 = bf16[4,64,128]{2,1,0:T(8,128)(2,1)} copy(bf16[4,64,128]{2,1,0:T(8,128)(2,1)} %bitcast.10) | data formatting | bytes 131072

commit v2 on v1

--- a/solution.py
+++ b/solution.py
@@ -43,15 +43,24 @@
     part_o,
     part_m,
     part_l,
+    away_o,
+    away_m,
+    away_l,
     own_w,
     own_v,
     send_buf,
     recv_buf,
+    last_send,
+    last_recv,
     local_sem,
     send_q,
     recv_q,
+    pass_send,
+    pass_recv,
     send_p,
     recv_p,
+    send_f,
+    recv_f,
 ):
     nblk, nbr, rdev, kvl, group, hd, keys, suf = cfg
     n = nblk * nbr
@@ -62,9 +71,6 @@
     my_blk = lax.axis_index("blk")
     my_br = lax.axis_index("branch")
     me = my_blk * nbr + my_br
-
-    def device(p):
-        return (grp, lax.div(p, nbr), lax.rem(p, nbr))
 
     pairs = [
         (q_hbm, q_own),
@@ -84,43 +90,89 @@
 
     barrier = pltpu.get_barrier_semaphore()
 
-    def greet(k, c):
+    half = nblk // 2
+    my_chip = lax.div(my_blk, 2)
+    my_core = lax.rem(my_blk, 2)
+
+    def near(d):
+        chip = lax.rem(my_chip + lax.div(d, 2), half)
+        return chip * 2 + lax.rem(my_core + lax.rem(d, 2), 2)
+
+    def along(k):
+        return lax.rem(my_br + k, nbr)
+
+    def ordered(t):
+        return jnp.where(t == nblk - 1, 1, t + 1)
+
+    def greet_branch(k, c):
         pl.semaphore_signal(
-            barrier, inc=1, device_id=device(lax.rem(me + k, n)), device_id_type=MESH
+            barrier, inc=1, device_id=(grp, my_blk, along(k)), device_id_type=MESH
         )
         return c
 
-    lax.fori_loop(1, n, greet, 0)
+    def greet_blk(d, c):
+        pl.semaphore_signal(barrier, inc=1, device_id=(grp, near(d), my_br), device_id_type=MESH)
+        return c
+
+    lax.fori_loop(1, nbr, greet_branch, 0)
+    lax.fori_loop(1, nblk, greet_blk, 0)
     for copy in local[:5]:
         copy.start()
     own_q.start()
     for copy in local[5:]:
         copy.start()
-    pl.semaphore_wait(barrier, n - 1)
-
-    def q_copy(p, source):
+    pl.semaphore_wait(barrier, nbr + nblk - 2)
+
+    def q_copy(j, source):
         return pltpu.make_async_remote_copy(
-            src_ref=q_hbm.at[:, lax.rem(p, nbr)],
-            dst_ref=q_all.at[pl.ds(source * rdev, rdev)],
-            send_sem=send_q.at[p],
+            src_ref=q_hbm.at[:, j],
+            dst_ref=q_all.at[pl.ds((my_blk * nbr + source) * rdev, rdev)],
+            send_sem=send_q.at[j],
             recv_sem=recv_q.at[source],
-            device_id=device(p),
+            device_id=(grp, my_blk, j),
             device_id_type=MESH,
         )
 
+    def pass_copy(ib, j, owner, src=None):
+        at = pl.ds((owner * nbr + j) * rdev, rdev)
+        return pltpu.make_async_remote_copy(
+            src_ref=q_all.at[at] if src is None else src,
+            dst_ref=q_all.at[at],
+            send_sem=pass_send.at[ib * nbr + j],
+            recv_sem=pass_recv.at[owner * nbr + j],
+            device_id=(grp, ib, my_br),
+            device_id_type=MESH,
+        )
+
     def send_one(k, c):
-        q_copy(lax.rem(me + k, n), me).start()
-        return c
-
-    lax.fori_loop(1, n, send_one, 0)
-
-    def p_copy(p, source):
+        q_copy(along(k), my_br).start()
+        return c
+
+    lax.fori_loop(1, nbr, send_one, 0)
+
+    def pass_own(t, c):
+        pass_copy(near(ordered(t)), my_br, my_blk, q_hbm.at[:, my_br]).start()
+        return c
+
+    lax.fori_loop(1, nblk, pass_own, 0)
+
+    def p_copy(ib, owner):
         return pltpu.make_async_remote_copy(
-            src_ref=send_buf.at[p],
-            dst_ref=recv_buf.at[source],
-            send_sem=send_p.at[p],
-            recv_sem=recv_p.at[source],
-            device_id=device(p),
+            src_ref=send_buf.at[pl.ds(ib * nbr, nbr)],
+            dst_ref=recv_buf.at[pl.ds(owner * nbr, nbr)],
+            send_sem=send_p.at[ib],
+            recv_sem=recv_p.at[owner],
+            device_id=(grp, ib, my_br),
+            device_id_type=MESH,
+        )
+
+    def f_copy(j, source):
+        return pltpu.make_async_remote_copy(
+            src_ref=last_send.at[j],
+            dst_ref=last_recv.at[source],
+            send_sem=send_f.at[j],
+            recv_sem=recv_f.at[source],
+            device_id=(grp, my_blk, j),
             device_id_type=MESH,
         )
 
@@ -172,34 +224,15 @@
         mid = rest.astype(BF16).astype(F32)
         return [high, mid, rest - mid]
 
-    def build(p, outs, tops, sums):
-        for h in range(kvl):
-            send_buf[p, h * mrow : (h + 1) * mrow, :] = outs[h].astype(BF16)
+    def build(buf, p, outs, tops, sums):
+        for h in range(kvl):
+            buf[p, h * mrow : (h + 1) * mrow, :] = outs[h].astype(BF16)
         stats = jnp.zeros((STAT_ROWS, hd), F32)
         for i, piece in enumerate(split(to_row(tops)) + split(to_row(sums))):
             stats = jnp.where(stat_line == i, piece, stats)
-        send_buf[p, kvl * mrow : kvl * mrow + STAT_ROWS, :] = stats.astype(BF16)
-
-    half = nblk // 2
-    my_chip = lax.div(my_blk, 2)
-    my_core = lax.rem(my_blk, 2)
-
-    def prefix_step(d, c):
-        chip = lax.rem(my_chip + lax.div(d, 2), half)
-        core = lax.rem(my_core + lax.rem(d, 2), 2)
-        ib = chip * 2 + core
-
-        @pl.when(d < nblk)
-        def _():
-            for jj in range(nbr):
-                q_copy(me, ib * nbr + jj).wait_recv()
-
-        @pl.when(d == nblk)
-        def _():
-            own_q.wait()
-            for k in range(1, nbr):
-                q_copy(me, my_blk * nbr + lax.rem(my_br + k, nbr)).wait_recv()
-
+        buf[p, kvl * mrow : kvl * mrow + STAT_ROWS, :] = stats.astype(BF16)
+
+    def attend(ib, keep_o, keep_m, keep_l):
         q_wide = q_all[pl.ds(ib * rows, rows)].astype(F32)
         for h in range(kvl):
             query = q_wide[:, h * group : (h + 1) * group, :].reshape(rows * group, hd)
@@ -209,26 +242,23 @@
             top = jnp.max(scores, axis=1, keepdims=True)
             weights = jnp.exp2((scores - top) * factor)
             total = jnp.sum(weights, axis=1, keepdims=True)
-            part_o[h] = jnp.dot(weights.astype(BF16), pv[h], preferred_element_type=F32)
-            part_m[h] = jnp.broadcast_to(top, (rows * group, hd))
-            part_l[h] = jnp.broadcast_to(total, (rows * group, hd))
-
-        @pl.when(d < nblk)
-        def _():
-            for jj in range(nbr):
-                at = slice(jj * mrow, (jj + 1) * mrow)
-                p = ib * nbr + jj
-                build(
-                    p,
-                    [part_o[h, at, :] for h in range(kvl)],
-                    [part_m[h, at, :] for h in range(kvl)],
-                    [part_l[h, at, :] for h in range(kvl)],
-                )
-                p_copy(p, me).start()
-
-        return c
-
-    lax.fori_loop(1, nblk + 1, prefix_step, 0)
+            keep_o[h] = jnp.dot(weights.astype(BF16), pv[h], preferred_element_type=F32)
+            keep_m[h] = jnp.broadcast_to(top, (rows * group, hd))
+            keep_l[h] = jnp.broadcast_to(total, (rows * group, hd))
+
+    def relay(k, c):
+        j = along(k)
+        q_copy(my_br, j).wait_recv()
+
+        def forward(t, c):
+            pass_copy(near(ordered(t)), j, my_blk).start()
+            return c
+
+        return lax.fori_loop(1, nblk, forward, c)
+
+    lax.fori_loop(1, nbr, relay, 0)
+    own_q.wait()
+    attend(my_blk, part_o, part_m, part_l)
 
     for copy in local[5:]:
         copy.wait()
@@ -240,8 +270,7 @@
     right_head = lax.rem(col, kvl) == row_head
     position = lax.div(col, kvl)
 
-    def suffix_step(k, c):
-        jj = lax.rem(my_br + k, nbr)
+    def suffix_step(jj, c):
         keep = []
         for r in range(rdev):
             b = jj * rdev + r
@@ -260,7 +289,6 @@
             total = jnp.sum(weights, axis=1, keepdims=True)
             out = jnp.dot(weights.astype(BF16), sv[slot], preferred_element_type=F32)
             done.append((out, jnp.broadcast_to(top, out.shape), jnp.broadcast_to(total, out.shape)))
-        outs, tops, sums = [], [], []
         at = pl.ds(pl.multiple_of(jj * mrow, mrow), mrow)
         for h in range(kvl):
             cut = slice(h * group, (h + 1) * group)
@@ -271,67 +299,124 @@
             top = jnp.maximum(m1, m2)
             one = jnp.exp2((m1 - top) * factor)
             two = jnp.exp2((m2 - top) * factor)
-            outs.append(o1 * one + o2 * two)
+            part_o[h, at, :] = o1 * one + o2 * two
+            part_m[h, at, :] = top
+            part_l[h, at, :] = l1 * one + l2 * two
+        return c
+
+    lax.fori_loop(0, nbr, suffix_step, 0)
+
+    def prefix_step(t, c):
+        ib = near(ordered(t))
+
+        def arrive(j, c):
+            pass_copy(my_blk, j, ib).wait_recv()
+            return c
+
+        lax.fori_loop(0, nbr, arrive, 0)
+        attend(ib, away_o, away_m, away_l)
+        for jj in range(nbr):
+            at = slice(jj * mrow, (jj + 1) * mrow)
+            build(
+                send_buf,
+                ib * nbr + jj,
+                [away_o[h, at, :] for h in range(kvl)],
+                [away_m[h, at, :] for h in range(kvl)],
+                [away_l[h, at, :] for h in range(kvl)],
+            )
+        p_copy(ib, my_blk).start()
+        return c
+
+    lax.fori_loop(1, nblk, prefix_step, 0)
+
+    def wait_one(d, c):
+        p_copy(my_blk, near(d)).wait_recv()
+        return c
+
+    lax.fori_loop(1, nblk, wait_one, 0)
+
+    def read_stats(buf, p):
+        block = buf[p, kvl * mrow : kvl * mrow + STAT_ROWS, :].astype(F32)
+        return (block[0:1] + block[1:2] + block[2:3], block[3:4] + block[4:5] + block[5:6])
+
+    def to_column(h, row):
+        return jnp.sum(jnp.where(picks[h], row, 0.0), axis=1, keepdims=True)
+
+    def gather(k, c):
+        jj = along(k)
+        at = pl.ds(pl.multiple_of(jj * mrow, mrow), mrow)
+        sources = [near(d) * nbr + jj for d in range(1, nblk)]
+        stats = [read_stats(recv_buf, p) for p in sources]
+        outs, tops, sums = [], [], []
+        for h in range(kvl):
+            heights = [to_column(h, item[0]) for item in stats]
+            mine = part_m[h, at, :]
+            top = mine
+            for height in heights:
+                top = jnp.maximum(top, height)
+            scale = jnp.exp2((mine - top) * factor)
+            num = part_o[h, at, :] * scale
+            den = part_l[h, at, :] * scale
+            for p, item, height in zip(sources, stats, heights):
+                scale = jnp.exp2((height - top) * factor)
+                num = num + recv_buf[p, h * mrow : (h + 1) * mrow, :].astype(F32) * scale
+                den = den + to_column(h, item[1]) * scale
+            outs.append(num)
             tops.append(top)
-            sums.append(l1 * one + l2 * two)
-        p = my_blk * nbr + jj
-        build(p, outs, tops, sums)
+            sums.append(den)
+        build(last_send, jj, outs, tops, sums)
 
         @pl.when(k < nbr)
         def _():
-            p_copy(p, me).start()
-
-        return c
-
-    lax.fori_loop(1, nbr + 1, suffix_step, 0)
-    recv_buf[me] = send_buf[me]
-
-    def wait_one(k, c):
-        p_copy(me, lax.rem(me + k, n)).wait_recv()
-        return c
-
-    lax.fori_loop(1, n, wait_one, 0)
-
-    def merge(jj, c):
+            f_copy(jj, my_br).start()
+
+        return c
+
+    lax.fori_loop(1, nbr + 1, gather, 0)
+    last_recv[my_br] = last_send[my_br]
+
+    def merge(k, c):
+        jj = along(k)
+
+        @pl.when(k > 0)
+        def _():
+            f_copy(my_br, jj).wait_recv()
+
+        row_top, row_sum = read_stats(last_recv, jj)
         finals = []
-        stats = []
-        for ii in range(nblk):
-            block = recv_buf[ii * nbr + jj, kvl * mrow : kvl * mrow + STAT_ROWS, :].astype(F32)
-            stats.append(
-                (block[0:1] + block[1:2] + block[2:3], block[3:4] + block[4:5] + block[5:6])
-            )
-        for h in range(kvl):
-            tops = [
-                jnp.sum(jnp.where(picks[h], s[0], 0.0), axis=1, keepdims=True) for s in stats
-            ]
-            sums = [
-                jnp.sum(jnp.where(picks[h], s[1], 0.0), axis=1, keepdims=True) for s in stats
-            ]
+        for h in range(kvl):
+            height = to_column(h, row_top)
             mine = own_w[jj, h]
-            top = mine
-            for t in tops:
-                top = jnp.maximum(top, t)
-            scale = jnp.exp2((mine - top) * factor)
-            num = own_v[jj, h] * scale
-            den = scale
-            for ii in range(nblk):
-                scale = jnp.exp2((tops[ii] - top) * factor)
-                piece = recv_buf[ii * nbr + jj, h * mrow : (h + 1) * mrow, :].astype(F32)
-                num = num + piece * scale
-                den = den + sums[ii] * scale
+            top = jnp.maximum(mine, height)
+            first_scale = jnp.exp2((mine - top) * factor)
+            scale = jnp.exp2((height - top) * factor)
+            piece = last_recv[jj, h * mrow : (h + 1) * mrow, :].astype(F32)
+            num = own_v[jj, h] * first_scale + piece * scale
+            den = first_scale + to_column(h, row_sum) * scale
             finals.append((num / den).reshape(rdev, group, hd))
         out_ref[:, jj] = jnp.concatenate(finals, axis=1).astype(BF16)
         return c
 
     lax.fori_loop(0, nbr, merge, 0)
 
-    def drain(k, c):
-        p = lax.rem(me + k, n)
-        q_copy(p, me).wait_send()
-        p_copy(p, me).wait_send()
-        return c
-
-    lax.fori_loop(1, n, drain, 0)
+    def drain_branch(k, c):
+        q_copy(along(k), my_br).wait_send()
+        f_copy(along(k), my_br).wait_send()
+        return c
+
+    lax.fori_loop(1, nbr, drain_branch, 0)
+
+    def drain_blk(d, c):
+        ib = near(d)
+
+        def drain_pass(j, c):
+            pass_copy(ib, j, my_blk).wait_send()
+            return c
+
+        p_copy(ib, my_blk).wait_send()
+        return lax.fori_loop(0, nbr, drain_pass, c)
+
+    lax.fori_loop(1, nblk, drain_blk, 0)
 
 
 def solution(mesh):
@@ -371,15 +456,24 @@
                 pltpu.VMEM((kvl, rows * group, hd), F32),
                 pltpu.VMEM((kvl, rows * group, hd), F32),
                 pltpu.VMEM((kvl, rows * group, hd), F32),
+                pltpu.VMEM((kvl, rows * group, hd), F32),
+                pltpu.VMEM((kvl, rows * group, hd), F32),
+                pltpu.VMEM((kvl, rows * group, hd), F32),
                 pltpu.VMEM((nbr, kvl, mrow, hd), F32),
                 pltpu.VMEM((nbr, kvl, mrow, hd), F32),
                 pltpu.VMEM((n, kvl * mrow + STAT_ROWS, hd), BF16),
                 pltpu.VMEM((n, kvl * mrow + STAT_ROWS, hd), BF16),
+                pltpu.VMEM((nbr, kvl * mrow + STAT_ROWS, hd), BF16),
+                pltpu.VMEM((nbr, kvl * mrow + STAT_ROWS, hd), BF16),
                 dma((10,)),
+                dma((nbr,)),
+                dma((nbr,)),
                 dma((n,)),
                 dma((n,)),
-                dma((n,)),
-                dma((n,)),
+                dma((nblk,)),
+                dma((nblk,)),
+                dma((nbr,)),
+                dma((nbr,)),
             ],
             compiler_params=pltpu.CompilerParams(
                 collective_id=0, has_side_effects=True, vmem_limit_bytes=60 * 1024 * 1024

time: 26.2 us -> 25.2 us (0.962)
  Pallas kernels: 24.6 us -> 23.5 us
    pallas_call x1, Pallas kernels: 24.6 us -> 23.5 us  [per_device(): pl.pallas_call(functools.partial(kernel, cfg), out_shape=jax.ShapeDtypeSt...]
where the time goes in v2:
time: 25.2 us; the launch traced here: 25 us
  Pallas kernels  23.5 us (93%)
  local copies, waits for them, and re-layouts  1.47 us (6%)
    pallas_call x1, Pallas kernels, per_device(): pl.pallas_call(functools.partial(kernel, cfg), out_shape=jax.ShapeDtypeSt...  23.5 us
    unnamed x1, local copies, waits for them, and re-layouts  1.47 us

profile of v2, /device:TPU:0, one launch (start us, length us, event | category | flops | bytes accessed | tf_op | source)
XLA Modules:
  0.0 25.0 jit_solution(8716011089378651894)
XLA Ops:
  0.0 23.5 %attend.1 = bf16[4,4,16,128]{3,2,1,0:T(8,128)(2,1)} custom-call(bf16[4,4,16,128]{3,2,1,0:T(8,128)(2,1)} %bitcast.11, bf16[4,8,128]{2,1,0:T(8,128)(2,1)} %nk_hbm.1, bf16[4,8,128]{2,1,0:T(8,128)(2,1)} %nv_hbm.1, bf16[4096,128]{1,0:T(8,128)(2,1)} %bitcast.8, bf16[4096,128]{1,0:T(8,128)(2,1)} %bitcast.9, bf16[16,1024,128]{2,1,0:T(8,128)(2,1)} %bitcast.6, ...), custom_call_target="tpu_custom_call" | custom-call | tf_op jit(solution)/shard_map/attend/pallas_call | solution.py:436
  23.5 1.5 %copy.11 = bf16[4,64,128]{2,1,0:T(8,128)(2,1)} copy(bf16[4,64,128]{2,1,0:T(8,128)(2,1)} %bitcast.10) | data formatting | bytes 131072
